TPU v7x, 32 devices: a whole 2x2x4 slice. The times are simulated.
32 devices in a mesh: seq: 8 (over z, y), chan: 4 (over x, core).
Axes of the slice: x: 2, y: 2, z: 4, core: 2. Of those that a mesh axis runs over, the one named last changes fastest.
Arguments:
- features: bfloat16 [2048, 3, 8192], P(('seq', 'chan')), may hold values from -6 to 6
- cotangent: bfloat16 [2048, 8192], P('seq', 'chan'), may hold values from -6 to 6
- short_filter: float32 [3, 512, 7], P(None, 'chan'), may hold values from -2.5 to 2.5
- medium_filter: float32 [512, 128], P('chan'), may hold values from -0.5 to 0.5
- doc_start: int32 [8], replicated, may hold values from 0 to 255
Outputs:
- hyena_out: bfloat16 [2048, 8192], P('seq', 'chan')
- feature_grad: bfloat16 [2048, 3, 8192], P(('seq', 'chan'))
Inputs may be any that keep to these rules, and one draw needn't show every extreme that they name: Each shard holds exactly one document start, at position doc_start[i] of its 256 positions.
All inputs are finite; a program needn't handle non-finite values.
Results may differ from a plain program's by a relative error of at most 0.006.
Values may be sent and summed in bfloat16 or wider, within the bound.
A program may use at most 128 MiB of HBM per device.

v0:
```python
import jax
import jax.numpy as jnp
from jax import lax
from jax.sharding import PartitionSpec as P

SHORT = 7
MEDIUM = 128
band_rows = 256


def from_behind(block, axis, distance):
    devices = range(lax.axis_size(axis))
    route = [(i - distance, i) for i in devices if i - distance in devices]
    return lax.ppermute(block, axis, route)


def segment_ids(positions, doc_start, shard_rows):
    bounds = jnp.arange(doc_start.shape[0], dtype=jnp.int32) * shard_rows + doc_start
    return jnp.sum((bounds[None, :] <= positions[:, None]).astype(jnp.int32), axis=1)


def short_forward(source, seg_ids, taps_full):
    row_count = source.shape[1] - (SHORT - 1)
    running = jnp.zeros((source.shape[0], row_count, source.shape[2]), jnp.float32)
    for offset in range(SHORT):
        row_start = SHORT - 1 - offset
        shifted = source[:, row_start : row_start + row_count]
        open_tap = seg_ids[row_start : row_start + row_count] == seg_ids[SHORT - 1 :]
        running = running + jnp.where(
            open_tap[None, :, None], taps_full[:, offset, :][:, None, :] * shifted, 0.0
        )
    return running


def short_backward(grad_short, seg_ids, taps_full):
    row_count = grad_short.shape[1]
    out_rows = row_count + SHORT - 1
    grad_padded = jnp.pad(grad_short, ((0, 0), (SHORT - 1, SHORT - 1), (0, 0)))
    seg_padded = jnp.concatenate([seg_ids, jnp.full((SHORT - 1,), -1, jnp.int32)])
    running = jnp.zeros((grad_short.shape[0], out_rows, grad_short.shape[2]), jnp.float32)
    for offset in range(SHORT):
        shifted = grad_padded[:, offset : offset + out_rows]
        open_tap = seg_ids == seg_padded[offset : offset + out_rows]
        running = running + jnp.where(
            open_tap[None, :, None], taps_full[:, offset, :][:, None, :] * shifted, 0.0
        )
    return running


def band_mats(filters_bf, seg_ids):
    lag_steps = (
        jnp.arange(band_rows, dtype=jnp.int32)[:, None]
        + MEDIUM
        - jnp.arange(band_rows + MEDIUM, dtype=jnp.int32)[None, :]
    )
    inside = (lag_steps >= 0) & (lag_steps < MEDIUM)
    lag_table = jnp.where(
        inside[None],
        jnp.take(filters_bf, jnp.clip(lag_steps, 0, MEDIUM - 1), axis=1),
        jnp.zeros((), filters_bf.dtype),
    )
    target_ids = seg_ids[MEDIUM : band_rows + MEDIUM]
    same_doc = target_ids[:, None] == seg_ids[None, :]
    matrices = [jnp.where(same_doc[None], lag_table, jnp.zeros((), lag_table.dtype))]
    return jnp.stack(matrices)


def body(features, cotangent, short_filter, medium_filter, doc_start):
    regrouped = lax.all_to_all(
        jnp.transpose(features, (1, 0, 2)), "chan", split_axis=2, concat_axis=1, tiled=True
    )
    shard_rows = regrouped.shape[1]
    local_width = regrouped.shape[2]
    local_groups = short_filter.shape[1]
    group_width = local_width // local_groups
    rim_reach = MEDIUM + SHORT - 1
    row_base = lax.axis_index("seq") * shard_rows
    positions = row_base - rim_reach + jnp.arange(shard_rows + rim_reach, dtype=jnp.int32)
    seg_all = segment_ids(positions, doc_start, shard_rows)
    taps_full = jnp.repeat(jnp.transpose(short_filter, (0, 2, 1)), group_width, axis=2)
    filters_bf = medium_filter.astype(jnp.bfloat16)
    before = from_behind(regrouped[:, shard_rows - rim_reach :], "seq", 1)
    extended = jnp.concatenate([before, regrouped], axis=1)
    short_ext = short_forward(extended, seg_all, taps_full)
    gated_ext = (short_ext[1] * short_ext[2]).astype(jnp.bfloat16)
    short_own = short_ext[:, MEDIUM:]
    blocks = shard_rows // band_rows
    window_rows = band_rows + MEDIUM
    matrices = band_mats(filters_bf, seg_all[SHORT - 1 :])
    windows = jnp.stack([gated_ext])
    windows = jnp.transpose(
        windows.reshape(blocks, window_rows, local_groups, group_width), (0, 2, 3, 1)
    )
    long_chan = jnp.einsum("bgts,bgcs->bgct", matrices, windows, preferred_element_type=jnp.float32)
    long_conv = jnp.transpose(long_chan, (0, 3, 1, 2)).reshape(shard_rows, local_width)
    query_short = short_own[0]
    key_short = short_own[1]
    value_short = short_own[2]
    hyena_out = (query_short * long_conv).astype(jnp.bfloat16)
    grad_query = cotangent * long_conv
    grad_long = (cotangent * query_short).astype(jnp.bfloat16)
    long_blocks = jnp.transpose(
        grad_long.reshape(blocks, band_rows, local_groups, group_width), (0, 2, 3, 1)
    )
    spread = jnp.einsum(
        "bgts,bgct->bgcs", matrices, long_blocks, preferred_element_type=jnp.float32
    )
    spread = jnp.transpose(spread, (0, 3, 1, 2)).reshape(blocks, window_rows, local_width)
    gated_grad = jnp.zeros((shard_rows + MEDIUM, local_width), jnp.float32)
    gated_grad = gated_grad.at[0:window_rows].add(spread[0])
    own_grad = gated_grad[MEDIUM:]
    seg_back = seg_all[MEDIUM:]
    head_grad = jnp.stack(
        [
            grad_query[: SHORT - 1],
            own_grad[: SHORT - 1] * value_short[: SHORT - 1],
            own_grad[: SHORT - 1] * key_short[: SHORT - 1],
        ],
        axis=0,
    )
    head_spread = short_backward(head_grad, seg_back[: 2 * (SHORT - 1)], taps_full)
    backward_out = jnp.concatenate(
        [gated_grad[:MEDIUM], head_spread[:, : SHORT - 1].reshape(3 * (SHORT - 1), local_width)],
        axis=0,
    )
    backward_in = from_behind(backward_out, "seq", -1)
    own_grad = own_grad.at[shard_rows - MEDIUM :].add(backward_in[:MEDIUM])
    grad_short = jnp.stack([grad_query, own_grad * value_short, own_grad * key_short], axis=0)
    spread_short = short_backward(grad_short, seg_back, taps_full)
    feature_full = (
        spread_short[:, SHORT - 1 :]
        .at[:, shard_rows - SHORT + 1 :]
        .add(backward_in[MEDIUM:].reshape(3, SHORT - 1, local_width))
    )
    restored = lax.all_to_all(
        feature_full.astype(jnp.bfloat16), "chan", split_axis=1, concat_axis=2, tiled=True
    )
    return (hyena_out, jnp.transpose(restored, (1, 0, 2)))


def solution(mesh):
    in_specs = (
        P(("seq", "chan"), None, None),
        P("seq", "chan"),
        P(None, "chan", None),
        P("chan", None),
        P(),
    )
    out_specs = (P("seq", "chan"), P(("seq", "chan"), None, None))
    return jax.shard_map(body, mesh=mesh, in_specs=in_specs, out_specs=out_specs, check_vma=False)
```

profile of v0, /device:TPU:0, one launch (start us, length us, event | category | flops | bytes accessed | tf_op | source)
XLA Modules:
  0.0 708.3 jit_solution(11230173101609217157)
XLA Ops:
  0.6 11.3 %copy.69 = bf16[64,3,8192]{0,1,2:T(4,128)(2,1)} copy(bf16[64,3,8192]{2,0,1:T(8,128)(2,1)} %param.13) | data formatting | bytes 6291456 | tf_op args[0]
  11.9 8.2 %bitcast_bitcast_fusion = bf16[8192,3,64]{2,1,0:T(4,128)(2,1)} fusion(bf16[64,3,8192]{0,1,2:T(4,128)(2,1)} %copy.69), kind=kLoop, calls=%fused_computation.145 | loop fusion | bytes 6291456
  20.1 8.6 %reshape.297 = bf16[4,2,196608]{2,1,0:T(2,128)(2,1)} reshape(bf16[8192,3,64]{2,1,0:T(4,128)(2,1)} %bitcast_bitcast_fusion) | data formatting | bytes 6291456
  28.7 4.2 all-to-all-start
  32.9 0.0 copy-done.26
  32.9 0.1 convert_reduce_fusion
  33.0 0.7 slice_compare_fusion.11
  33.7 0.5 slice.338
  34.2 1.6 broadcast_in_dim.198
  35.7 2.1 reshape.280
  37.9 0.8 fusion.59
  38.6 0.9 compare_select_fusion
  39.6 1.0 reshape.290
  40.6 0.8 broadcast_clamp_fusion
  41.4 28.5 %all-to-all-done = bf16[4,2,196608]{2,1,0:T(2,128)(2,1)S(1)} async-done(((bf16[4,2,196608]{2,1,0:T(2,128)(2,1)}), bf16[4,2,196608]{2,1,0:T(2,128)(2,1)S(1)}, u32[]{:S(2)}, u32[]{:S(2)}) %all-to-all-start) | async-done | bytes 3145760 | tf_op jit(solution)/shard_map/all_to_all | solution.py:69
  69.9 6.4 reshape.298
  76.4 10.7 %copy.71 = bf16[3,4,64,2048]{3,2,1,0:T(8,128)(2,1)S(1)} copy(bf16[3,4,64,2048]{2,0,3,1:T(4,128)(2,1)} %bitcast.101) | data formatting | bytes 6291456 | tf_op jit(solution)/shard_map/all_to_all | solution.py:69
  87.0 1.6 slice.375
  88.6 5.4 collective-permute-start
  94.1 0.6 slice_compare_fusion.16
  94.7 0.1 slice.305
  94.8 0.1 slice.326
  94.9 0.1 copy.73
  95.0 372.4 %gather_fusion = bf16[98304,128]{1,0:T(8,128)(2,1)} fusion(bf16[128,128]{0,1:T(8,128)(2,1)S(1)} %copy.73, s32[98304]{0:T(1024)} %broadcast_clamp_fusion), kind=kCustom, calls=%fused_computation | custom fusion | bytes 50724864 | tf_op jit(solution)/shard_map/jit(_take)/gather | solution.py:59
  467.4 32.0 %copy.74 = bf16[256,384,128]{1,0,2:T(8,128)(2,1)} copy(bf16[256,384,128]{2,1,0:T(8,128)(2,1)} %bitcast.100) | data formatting | bytes 50331648 | tf_op jit(solution)/shard_map/jit(_take)/gather | solution.py:59
  499.5 1.0 fusion.43
  500.6 0.0 collective-permute-done
  500.7 44.8 %select_add_fusion = f32[3,384,2048]{2,1,0:T(8,128)S(1)} fusion(bf16[3,256,2048]{2,1,0:T(8,128)(2,1)S(1)} %bitcast.103, bf16[3,134,2048]{2,1,0:T(8,128)(2,1)} %collective-permute-done, f32[3,2048]{1,0:T(4,128)S(1)} %get-tuple-element.91, f32[3,2048]{1,0:T(4,128)S(1)} %get-tuple-element.92, f32[3,2048]{1,0:T(4,128)S(1)} %get-tuple-element.93, ...), kind=kLoop, calls=%fused_computation.18 | loop fusion | flops 110886912 | bytes 14403840 | tf_op jit(solution)/shard_map/add | solution.py:29
  545.5 3.5 copy-done
  549.1 0.4 fusion.27
  549.5 0.9 copy.72
  550.4 12.9 %fusion.2 = f32[128,16,256]{2,1,0:T(8,128)} fusion(bf16[128,16,384]{2,1,0:T(8,128)(2,1)S(1)} %bitcast.112, bf16[256,384,128]{1,0,2:T(8,128)(2,1)} %copy.74, pred[256,384]{1,0:T(8,128)(4,1)} %get-tuple-element.97, pred[256,384]{1,0:T(8,128)(4,1)} %get-tuple-element.84, pred[256,384]{1,0:T(8,128)(4,1)S(1)} %get-tuple-element.83), kind=kOutput, calls=%fused_computation.3 | convolution fusion | flops 440401920 | bytes 29130752 | tf_op jit(solution)/shard_map/bgts,bgcs->bgct/dot_general | solution.py:94
  563.3 1.9 copy.75
  565.2 3.8 convert_multiply_fusion.1
  569.0 1.5 copy.77
  570.5 16.5 %fusion.33 = f32[1,384,128,16]{1,3,2,0:T(8,128)} fusion(bf16[128,16,256]{2,1,0:T(8,128)(2,1)} %bitcast.113, bf16[256,384,128]{1,0,2:T(8,128)(2,1)} %copy.74, pred[256,384]{1,0:T(8,128)(4,1)S(1)} %get-tuple-element.83, pred[256,384]{1,0:T(8,128)(4,1)} %get-tuple-element.84, pred[256,384]{1,0:T(8,128)(4,1)} %get-tuple-element.97), kind=kOutput, calls=%fused_computation.67 | convolution fusion | flops 440401920 | bytes 29655040 | tf_op jit(solution)/shard_map/bgts,bgct->bgcs/dot_general | solution.py:105
  587.0 3.1 fusion.58
  590.1 0.9 copy.78
  591.0 0.9 slice_multiply_fusion.16
  592.0 0.8 slice_bitcast_fusion.3
  592.8 0.1 select_maximum_fusion.2
  592.9 0.3 slice_multiply_fusion.10
  593.3 0.2 fusion.46
  593.6 1.6 copy.80
  595.1 1.1 pad_maximum_fusion.1
  596.2 1.3 collective-permute-start.1
  597.6 0.1 slice_compare_fusion.5
  597.6 3.1 slice.397
  600.8 3.1 copy.82
  603.8 1.6 copy.81
  605.4 21.7 %collective-permute-done.1 = f32[146,2048]{1,0:T(8,128)} collective-permute-done((f32[146,2048]{1,0:T(8,128)}, f32[146,2048]{1,0:T(8,128)}, u32[]{:S(2)}, u32[]{:S(2)}) %collective-permute-start.1) | collective-permute-done | bytes 1196064 | tf_op jit(solution)/shard_map/ppermute | solution.py:14
  627.1 2.3 fusion.36
  629.4 5.4 fusion.32
  634.8 1.5 select_maximum_fusion
  636.3 8.0 %fusion.10 = f32[3,262,2048]{2,1,0:T(8,128)S(1)} fusion(f32[3,268,2048]{2,1,0:T(8,128)S(1)} %select_maximum_fusion, f32[3,2048]{1,0:T(4,128)S(1)} %get-tuple-element.91, f32[3,2048]{1,0:T(4,128)S(1)} %get-tuple-element.92, f32[3,2048]{1,0:T(4,128)S(1)} %get-tuple-element.93, f32[3,2048]{1,0:T(4,128)S(1)} %copy-done.4, f32[3,2048]{1,0:T(4,128)S(1)} %get-tuple-element.95, ...), kind=kLoop, calls=%fused_computation.24 | loop fusion | flops 30584832 | bytes 51684900 | tf_op jit(solution)/shard_map/add | solution.py:44
  644.4 2.7 copy-done.1
  647.1 0.9 slice.433
  648.0 0.9 slice.435
  649.0 1.0 slice_add_fusion.1
  649.9 0.3 scatter-add.9
  650.3 2.7 copy.83
  653.0 50.7 %all_to_all.36 = bf16[3,256,2048]{2,0,1:T(4,128)(2,1)S(1)} all-to-all(bf16[3,256,2048]{2,0,1:T(4,128)(2,1)S(1)} %copy.83), channel_id=1, replica_groups=mesh['seq'=8,'chan'=4] {'chan'}, dimensions={1} | all-to-all | bytes 6291456 | tf_op jit(solution)/shard_map/all_to_all | solution.py:135
  703.7 2.3 copy.84
  706.0 2.1 copy.95
  (63 shorter events, 0.3 us)
Async XLA Ops:
  20.0 12.9 %copy-start.26 = (s32[8]{0:T(128)S(1)}, s32[8]{0:T(128)}, u32[]{:S(2)}) copy-start(s32[8]{0:T(128)} %param.17) | copy-start | bytes 100
  20.1 14.1 %copy-start.15 = (f32[3,128,7]{1,2,0:T(8,128)S(1)}, f32[3,128,7]{1,2,0:T(8,128)}, u32[]{:S(2)}) copy-start(f32[3,128,7]{1,2,0:T(8,128)} %param.15) | copy-start | bytes 32260
  28.7 41.2 %all-to-all-start = ((bf16[4,2,196608]{2,1,0:T(2,128)(2,1)}), bf16[4,2,196608]{2,1,0:T(2,128)(2,1)S(1)}, u32[]{:S(2)}, u32[]{:S(2)}) async-start(bf16[4,2,196608]{2,1,0:T(2,128)(2,1)} %reshape.297), calls=%async_computation | async-start | bytes 6291456 | tf_op jit(solution)/shard_map/all_to_all | solution.py:69
  33.0 61.8 %copy-start.5 = (s32[390]{0:T(512)}, s32[390]{0:T(512)S(1)}, u32[]{:S(2)}) copy-start(s32[390]{0:T(512)S(1)} %convert_reduce_fusion) | copy-start | bytes 4684
  76.3 17.7 %copy-start.25 = (s32[12]{0:T(128)S(1)}, s32[12]{0:T(128)}, u32[]{:S(2)}) copy-start(s32[12]{0:T(128)} %slice.338) | copy-start | bytes 148
  76.3 18.5 %copy-start.13 = (f32[3,1,2048]{2,1,0:T(1,128)S(1)}, f32[3,1,2048]{2,1,0:T(1,128)}, u32[]{:S(2)}) copy-start(f32[3,1,2048]{2,1,0:T(1,128)} %get-tuple-element.64) | copy-start | bytes 73732
  76.4 18.5 %copy-start.14 = (f32[128,128]{1,0:T(8,128)S(1)}, f32[128,128]{1,0:T(8,128)}, u32[]{:S(2)}) copy-start(f32[128,128]{1,0:T(8,128)} %param.16) | copy-start | bytes 196612
  88.6 412.0 %collective-permute-start = (bf16[3,134,2048]{2,1,0:T(8,128)(2,1)}, bf16[3,134,2048]{2,1,0:T(8,128)(2,1)}, u32[]{:S(2)}, u32[]{:S(2)}) collective-permute-start(bf16[3,134,2048]{2,1,0:T(8,128)(2,1)} %slice.375), channel_id=1, source_target_pairs={{0,4},{4,8},{8,12},{12,16},{16,20},{20,24},{24,28},{1,5},{5,9},{9,... | collective-permute-start | bytes 4939784 | tf_op jit(solution)/shard_map/ppermute | solution.py:14
  467.4 33.1 %copy-start.11 = (f32[3,1,2048]{2,1,0:T(1,128)S(1)}, f32[3,1,2048]{2,1,0:T(1,128)}, u32[]{:S(2)}) copy-start(f32[3,1,2048]{2,1,0:T(1,128)} %get-tuple-element.65) | copy-start | bytes 73732
  467.4 33.1 %copy-start.12 = (f32[3,1,2048]{2,1,0:T(1,128)S(1)}, f32[3,1,2048]{2,1,0:T(1,128)}, u32[]{:S(2)}) copy-start(f32[3,1,2048]{2,1,0:T(1,128)} %get-tuple-element.66) | copy-start | bytes 73732
  467.4 33.1 %copy-start.9 = (f32[3,1,2048]{2,1,0:T(1,128)S(1)}, f32[3,1,2048]{2,1,0:T(1,128)}, u32[]{:S(2)}) copy-start(f32[3,1,2048]{2,1,0:T(1,128)} %get-tuple-element.67) | copy-start | bytes 73732
  467.4 33.2 %copy-start.10 = (f32[3,1,2048]{2,1,0:T(1,128)S(1)}, f32[3,1,2048]{2,1,0:T(1,128)}, u32[]{:S(2)}) copy-start(f32[3,1,2048]{2,1,0:T(1,128)} %get-tuple-element.68) | copy-start | bytes 73732
  467.4 33.2 %copy-start.7 = (f32[3,1,2048]{2,1,0:T(1,128)S(1)}, f32[3,1,2048]{2,1,0:T(1,128)}, u32[]{:S(2)}) copy-start(f32[3,1,2048]{2,1,0:T(1,128)} %get-tuple-element.69) | copy-start | bytes 73732
  467.4 33.2 %copy-start.8 = (f32[3,1,2048]{2,1,0:T(1,128)S(1)}, f32[3,1,2048]{2,1,0:T(1,128)}, u32[]{:S(2)}) copy-start(f32[3,1,2048]{2,1,0:T(1,128)} %get-tuple-element.70) | copy-start | bytes 73732
  467.4 33.2 %copy-start.22 = (pred[384]{0:T(512)(128)(4,1)S(1)}, pred[384]{0:T(512)(128)(4,1)}, u32[]{:S(2)}) copy-start(pred[384]{0:T(512)(128)(4,1)} %get-tuple-element.79) | copy-start | bytes 1156
  467.4 33.2 %copy-start.23 = (pred[384]{0:T(512)(128)(4,1)S(1)}, pred[384]{0:T(512)(128)(4,1)}, u32[]{:S(2)}) copy-start(pred[384]{0:T(512)(128)(4,1)} %get-tuple-element.80) | copy-start | bytes 1156
  467.4 33.2 %copy-start.24 = (pred[384]{0:T(512)(128)(4,1)S(1)}, pred[384]{0:T(512)(128)(4,1)}, u32[]{:S(2)}) copy-start(pred[384]{0:T(512)(128)(4,1)} %get-tuple-element.81) | copy-start | bytes 1156
  500.6 92.7 %copy-start.3 = (f32[3,2048]{1,0:T(4,128)}, f32[3,2048]{1,0:T(4,128)S(1)}, u32[]{:S(2)}) copy-start(f32[3,2048]{1,0:T(4,128)S(1)} %get-tuple-element.94) | copy-start | bytes 73732
  545.5 3.5 copy-start
  586.9 3.1 slice-start
  586.9 5.9 copy-start.21
  586.9 6.3 copy-start.16
  586.9 6.3 copy-start.17
  587.0 6.3 copy-start.18
  587.0 6.3 copy-start.19
  587.0 6.3 copy-start.20
  592.8 4.7 copy-start.6
  596.2 30.8 %collective-permute-start.1 = (f32[146,2048]{1,0:T(8,128)}, f32[146,2048]{1,0:T(8,128)}, u32[]{:S(2)}, u32[]{:S(2)}) collective-permute-start(f32[146,2048]{1,0:T(8,128)} %pad_maximum_fusion.1), channel_id=1, source_target_pairs={{4,0},{8,4},{12,8},{16,12},{20,16},{24,20},{28,24},{5,1},{9,5},{13... | collective-permute-start | bytes 3588104 | tf_op jit(solution)/shard_map/ppermute | solution.py:14
  629.4 5.4 copy-start.2
  634.8 1.5 copy-start.4
  644.4 2.7 copy-start.1
where the time goes:
time: 722 us; the launch traced here: 708 us
  local copies, waits for them, and re-layouts  492 us (68%)
  other arithmetic  74.1 us (10%)
  blocking collectives  50.7 us (7%)
  waiting for transfers between devices  50.2 us (7%)
  matrix products  29.4 us (4%)
  starting transfers between devices  10.9 us (2%)
    gather x2, local copies, waits for them, and re-layouts, band_mats(): jnp.take(filters_bf, jnp.clip(lag_steps, 0, MEDIUM - 1), axis=1)  404 us
    all_to_all x1, blocking collectives, body(): lax.all_to_all(feature_full.astype(jnp.bfloat16), 'chan', split_axis=1, c...  50.7 us
    add x1, other arithmetic, short_forward(): running + jnp.where(open_tap[None, :, None], taps_full[:, offset, :][:, N...  44.8 us
    unnamed x63, local copies, waits for them, and re-layouts  41.1 us
    all_to_all x1, waiting for transfers between devices, body(): lax.all_to_all(jnp.transpose(features, (1, 0, 2)), 'chan', split_axis=2,...  28.5 us
    ppermute x2, waiting for transfers between devices, from_behind(): return lax.ppermute(block, axis, route)  21.7 us
    dot_general x1, matrix products, body(): jnp.einsum('bgts,bgct->bgcs', matrices, long_blocks, preferred_element_ty...  16.5 us
  transfers between devices with their start and end apart: 3, of which 2 were waited for; matrix products, arithmetic and copies ran while one was open for 60% of the time, Pallas kernels for 0%

commit v1 on v0

--- a/solution.py
+++ b/solution.py
@@ -66,9 +66,11 @@
 
 
 def body(features, cotangent, short_filter, medium_filter, doc_start):
-    regrouped = lax.all_to_all(
-        jnp.transpose(features, (1, 0, 2)), "chan", split_axis=2, concat_axis=1, tiled=True
-    )
+    x = jnp.transpose(features, (1, 0, 2))
+    size = lax.axis_size("chan")
+    shards = jnp.stack(jnp.split(x, size, axis=2), axis=0)
+    shards = lax.all_to_all(shards, "chan", split_axis=0, concat_axis=0)
+    regrouped = jnp.concatenate(shards, axis=1)
     shard_rows = regrouped.shape[1]
     local_width = regrouped.shape[2]
     local_groups = short_filter.shape[1]

time: 722 us -> 678 us (0.939)
  local copies, waits for them, and re-layouts: 492 us -> 445 us
    unnamed x63 -> x37, local copies, waits for them, and re-layouts: 41.1 us -> 6.55 us
    all_to_all x1, local copies, waits for them, and re-layouts: 10.7 us -> 2.11 us  [body(): shards = lax.all_to_all(shards, 'chan', split_axis=0, concat_axis=0)]
  transfers between devices with their start and end apart: 3 -> 3, of which waited for: 2 -> 2; matrix products, arithmetic and copies ran while one was open for 60% -> 62% of each run, Pallas kernels for 0% -> 0%
where the time goes in v1:
time: 678 us; the launch traced here: 670 us
  local copies, waits for them, and re-layouts  445 us (66%)
  other arithmetic  75.6 us (11%)
  waiting for transfers between devices  56.3 us (8%)
  blocking collectives  50.7 us (7%)
  matrix products  29.3 us (4%)
  starting transfers between devices  11.4 us (2%)
    gather x2, local copies, waits for them, and re-layouts, band_mats(): jnp.take(filters_bf, jnp.clip(lag_steps, 0, MEDIUM - 1), axis=1)  404 us
    all_to_all x1, blocking collectives, body(): lax.all_to_all(feature_full.astype(jnp.bfloat16), 'chan', split_axis=1, c...  50.7 us
    add x1, other arithmetic, short_forward(): running + jnp.where(open_tap[None, :, None], taps_full[:, offset, :][:, N...  45.1 us
    all_to_all x1, waiting for transfers between devices, body(): shards = lax.all_to_all(shards, 'chan', split_axis=0, concat_axis=0)  34.4 us
    ppermute x2, waiting for transfers between devices, from_behind(): return lax.ppermute(block, axis, route)  21.9 us
    dot_general x1, matrix products, body(): jnp.einsum('bgts,bgct->bgcs', matrices, long_blocks, preferred_element_ty...  16.5 us
  transfers between devices with their start and end apart: 3, of which 2 were waited for; matrix products, arithmetic and copies ran while one was open for 62% of the time, Pallas kernels for 0%

profile of v1, /device:TPU:0, one launch (start us, length us, event | category | flops | bytes accessed | tf_op | source)
XLA Modules:
  0.0 669.7 jit_solution(9376648761500305445)
XLA Ops:
  0.6 2.1 slice_bitcast_fusion.6
  2.7 0.0 copy-start.15
  2.7 0.0 copy-start.8
  2.7 1.9 pad_maximum_fusion.1
  4.6 4.7 all-to-all-start
  9.3 0.0 copy-done.15
  9.3 0.1 convert_reduce_fusion
  9.4 0.7 slice_compare_fusion.11
  10.1 0.0 copy-done.8
  10.1 0.4 broadcast_in_dim.198
  10.5 0.0 copy-start.7
  10.5 0.8 reshape.286
  11.3 0.1 fusion.59
  11.5 0.2 compare_select_fusion
  11.7 0.8 broadcast_clamp_fusion
  12.5 34.4 %all-to-all-done = bf16[4,3,64,2048]{3,2,1,0:T(8,128)(2,1)} async-done(((bf16[4,3,64,2048]{3,2,1,0:T(8,128)(2,1)}), bf16[4,3,64,2048]{3,2,1,0:T(8,128)(2,1)}, u32[]{:S(2)}, u32[]{:S(2)}) %all-to-all-start) | async-done | bytes 3145760 | tf_op jit(solution)/shard_map/all_to_all | solution.py:72
  46.9 2.1 copy.72
  49.0 1.6 slice.375
  50.5 5.5 collective-permute-start
  56.0 0.7 slice_compare_fusion.16
  56.7 0.1 slice.305
  56.8 0.1 slice.326
  56.9 0.1 copy.74
  57.0 372.0 %gather_fusion = bf16[98304,128]{1,0:T(8,128)(2,1)} fusion(bf16[128,128]{0,1:T(8,128)(2,1)S(1)} %copy.74, s32[98304]{0:T(1024)} %broadcast_clamp_fusion), kind=kCustom, calls=%fused_computation | custom fusion | bytes 50724864 | tf_op jit(solution)/shard_map/jit(_take)/gather | solution.py:59
  429.0 32.2 %copy.75 = bf16[256,384,128]{1,0,2:T(8,128)(2,1)} copy(bf16[256,384,128]{2,1,0:T(8,128)(2,1)} %bitcast.102) | data formatting | bytes 50331648 | tf_op jit(solution)/shard_map/jit(_take)/gather | solution.py:59
  461.2 1.0 fusion.43
  462.3 0.0 collective-permute-done
  462.3 45.1 %select_add_fusion = f32[3,384,2048]{2,1,0:T(8,128)S(1)} fusion(bf16[3,256,2048]{2,1,0:T(8,128)(2,1)S(1)} %bitcast.104, bf16[3,134,2048]{2,1,0:T(8,128)(2,1)} %collective-permute-done, f32[3,2048]{1,0:T(4,128)S(1)} %get-tuple-element.95, f32[3,2048]{1,0:T(4,128)S(1)} %get-tuple-element.96, f32[3,2048]{1,0:T(4,128)S(1)} %get-tuple-element.97, ...), kind=kLoop, calls=%fused_computation.18 | loop fusion | flops 110886912 | bytes 14403840 | tf_op jit(solution)/shard_map/add | solution.py:29
  507.4 3.6 copy-done
  511.0 0.4 fusion.27
  511.4 0.9 copy.73
  512.3 12.8 %fusion.2 = f32[128,16,256]{2,1,0:T(8,128)} fusion(bf16[128,16,384]{2,1,0:T(8,128)(2,1)S(1)} %bitcast.114, bf16[256,384,128]{1,0,2:T(8,128)(2,1)} %copy.75, pred[256,384]{1,0:T(8,128)(4,1)} %get-tuple-element.101, pred[256,384]{1,0:T(8,128)(4,1)} %get-tuple-element.88, pred[256,384]{1,0:T(8,128)(4,1)S(1)} %get-tuple-element.87), kind=kOutput, calls=%fused_computation.3 | convolution fusion | flops 440401920 | bytes 29130752 | tf_op jit(solution)/shard_map/bgts,bgcs->bgct/dot_general | solution.py:96
  525.1 1.9 copy.76
  527.0 3.7 convert_multiply_fusion.1
  530.8 1.3 copy.78
  532.1 16.5 %fusion.33 = f32[1,384,128,16]{1,3,2,0:T(8,128)} fusion(bf16[128,16,256]{2,1,0:T(8,128)(2,1)} %bitcast.115, bf16[256,384,128]{1,0,2:T(8,128)(2,1)} %copy.75, pred[256,384]{1,0:T(8,128)(4,1)S(1)} %get-tuple-element.87, pred[256,384]{1,0:T(8,128)(4,1)} %get-tuple-element.88, pred[256,384]{1,0:T(8,128)(4,1)} %get-tuple-element.101), kind=kOutput, calls=%fused_computation.68 | convolution fusion | flops 440401920 | bytes 29655040 | tf_op jit(solution)/shard_map/bgts,bgct->bgcs/dot_general | solution.py:107
  548.6 3.1 fusion.58
  551.7 0.9 copy.79
  552.6 0.9 slice_multiply_fusion.16
  553.6 0.8 slice_bitcast_fusion.7
  554.4 0.1 select_maximum_fusion.2
  554.5 0.3 slice_multiply_fusion.10
  554.9 0.2 fusion.46
  555.2 1.6 copy.81
  556.7 1.2 pad_maximum_fusion.2
  557.9 1.3 collective-permute-start.1
  559.2 0.1 slice_compare_fusion.5
  559.3 3.1 slice.397
  562.4 2.9 copy.83
  565.3 1.6 copy.82
  566.9 21.9 %collective-permute-done.1 = f32[146,2048]{1,0:T(8,128)} collective-permute-done((f32[146,2048]{1,0:T(8,128)}, f32[146,2048]{1,0:T(8,128)}, u32[]{:S(2)}, u32[]{:S(2)}) %collective-permute-start.1) | collective-permute-done | bytes 1196064 | tf_op jit(solution)/shard_map/ppermute | solution.py:14
  588.7 2.3 fusion.36
  591.0 5.4 fusion.32
  596.5 1.5 select_maximum_fusion
  598.0 8.0 %fusion.10 = f32[3,262,2048]{2,1,0:T(8,128)S(1)} fusion(f32[3,268,2048]{2,1,0:T(8,128)S(1)} %select_maximum_fusion, f32[3,2048]{1,0:T(4,128)S(1)} %get-tuple-element.95, f32[3,2048]{1,0:T(4,128)S(1)} %get-tuple-element.96, f32[3,2048]{1,0:T(4,128)S(1)} %get-tuple-element.97, f32[3,2048]{1,0:T(4,128)S(1)} %copy-done.4, f32[3,2048]{1,0:T(4,128)S(1)} %get-tuple-element.99, ...), kind=kLoop, calls=%fused_computation.24 | loop fusion | flops 30584832 | bytes 51684900 | tf_op jit(solution)/shard_map/add | solution.py:44
  606.0 2.7 copy-done.1
  608.8 0.9 slice.433
  609.7 0.9 slice.435
  610.6 1.0 slice_add_fusion.1
  611.6 0.3 scatter-add.9
  611.9 2.7 copy.84
  614.6 50.7 %all_to_all.23 = bf16[3,256,2048]{2,0,1:T(4,128)(2,1)S(1)} all-to-all(bf16[3,256,2048]{2,0,1:T(4,128)(2,1)S(1)} %copy.84), channel_id=1, replica_groups=mesh['seq'=8,'chan'=4] {'chan'}, dimensions={1} | all-to-all | bytes 6291456 | tf_op jit(solution)/shard_map/all_to_all | solution.py:137
  665.4 2.3 copy.85
  667.6 2.1 copy.94
  (39 shorter events, 0.2 us)
Async XLA Ops:
  2.7 6.6 copy-start.15
  2.7 7.4 %copy-start.8 = (f32[3,128,7]{1,2,0:T(8,128)S(1)}, f32[3,128,7]{1,2,0:T(8,128)}, u32[]{:S(2)}) copy-start(f32[3,128,7]{1,2,0:T(8,128)} %param.15) | copy-start | bytes 32260
  4.6 42.2 %all-to-all-start = ((bf16[4,3,64,2048]{3,2,1,0:T(8,128)(2,1)}), bf16[4,3,64,2048]{3,2,1,0:T(8,128)(2,1)}, u32[]{:S(2)}, u32[]{:S(2)}) async-start(bf16[4,3,64,2048]{3,2,1,0:T(8,128)(2,1)} %pad_maximum_fusion.1), calls=%async_computation | async-start | bytes 6291456 | tf_op jit(solution)/shard_map/all_to_all | solution.py:72
  9.4 47.4 %copy-start.5 = (s32[390]{0:T(512)}, s32[390]{0:T(512)S(1)}, u32[]{:S(2)}) copy-start(s32[390]{0:T(512)S(1)} %convert_reduce_fusion) | copy-start | bytes 4684
  10.5 46.4 %copy-start.7 = (f32[128,128]{1,0:T(8,128)S(1)}, f32[128,128]{1,0:T(8,128)}, u32[]{:S(2)}) copy-start(f32[128,128]{1,0:T(8,128)} %param.16) | copy-start | bytes 196612
  50.5 411.8 %collective-permute-start = (bf16[3,134,2048]{2,1,0:T(8,128)(2,1)}, bf16[3,134,2048]{2,1,0:T(8,128)(2,1)}, u32[]{:S(2)}, u32[]{:S(2)}) collective-permute-start(bf16[3,134,2048]{2,1,0:T(8,128)(2,1)} %slice.375), channel_id=1, source_target_pairs={{0,4},{4,8},{8,12},{12,16},{16,20},{20,24},{24,28},{1,5},{5,9},{9,... | collective-permute-start | bytes 4939784 | tf_op jit(solution)/shard_map/ppermute | solution.py:14
  462.3 92.6 %copy-start.3 = (f32[3,2048]{1,0:T(4,128)}, f32[3,2048]{1,0:T(4,128)S(1)}, u32[]{:S(2)}) copy-start(f32[3,2048]{1,0:T(4,128)S(1)} %get-tuple-element.98) | copy-start | bytes 73732
  507.4 3.6 copy-start
  548.6 3.1 slice-start
  548.6 5.9 copy-start.14
  548.6 6.3 copy-start.9
  548.6 6.3 copy-start.10
  548.6 6.3 copy-start.11
  548.6 6.3 copy-start.12
  548.6 6.3 copy-start.13
  554.4 4.8 copy-start.6
  557.9 30.8 %collective-permute-start.1 = (f32[146,2048]{1,0:T(8,128)}, f32[146,2048]{1,0:T(8,128)}, u32[]{:S(2)}, u32[]{:S(2)}) collective-permute-start(f32[146,2048]{1,0:T(8,128)} %pad_maximum_fusion.2), channel_id=1, source_target_pairs={{4,0},{8,4},{12,8},{16,12},{20,16},{24,20},{28,24},{5,1},{9,5},{13... | collective-permute-start | bytes 3588104 | tf_op jit(solution)/shard_map/ppermute | solution.py:14
  591.0 5.4 copy-start.2
  596.5 1.5 copy-start.4
  606.0 2.7 copy-start.1
